TPU v7x, 32 devices: a whole 2x2x4 slice. The times are simulated.
32 devices in a mesh: ens: 2 (over y), lon: 4 (over z), dom: 4 (over x, core).
Axes of the slice: x: 2, y: 2, z: 4, core: 2. Of those that a mesh axis runs over, the one named last changes fastest.
Arguments:
- particles: bfloat16 [16, 69, 96, 256], P(('ens', 'dom'), None, 'lon'), parts along dimension 0, may hold values from -6 to 6
- observed: bfloat16 [138, 96, 256], P('ens', 'lon'), parts along dimension 0, may hold values from -6 to 6
- precision: float32 [192, 256], P(('ens', 'lon')), parts along dimension 0, may hold values from 0.25 to 12, as said below
- stations: int32 [192, 256], P(('ens', 'lon')), parts along dimension 0, may hold values 0 or 1
- ancestors: int32 [16], P(('ens', 'dom')), parts along dimension 0, may hold values from 0 to 7
- tempering: float32 [2], P('ens'), parts along dimension 0, may hold values from 1 to 4
- w_in: bfloat16 [3, 3, 64, 69], replicated, may hold values from -0.25 to 0.25
- w_mid: bfloat16 [3, 3, 64, 64], replicated, may hold values from -0.25 to 0.25
- w_out: bfloat16 [3, 3, 69, 64], replicated, may hold values from -0.25 to 0.25
Outputs:
- new_particles: bfloat16 [16, 69, 96, 256], P(('ens', 'dom'), None, 'lon'), parts along dimension 0
- weights: float32 [16], P(('ens', 'dom')), parts along dimension 0
There are 2 independent parts, one for each index of `ens`. A program takes and returns all parts, laid end to end along the dimension named above; an argument that names none is the same for every part. Nothing has to cross between parts.
Inputs may be any that keep to these rules, and one draw needn't show every extreme that they name: `precision`: positive everywhere; no other structure is promised. Slot s continues particle ancestors[s]; a particle may be continued by several slots or by none.
All inputs are finite; a program needn't handle non-finite values. No bound on the sum of `stations` on one device may be relied on, other than what follows from the above.
Results may differ from a plain program's by a relative error of at most 0.0021.
Values may be sent and summed in bfloat16 or wider, within the bound.
A program may use at most 128 MiB of HBM per device.

v0:
```python
import jax
import jax.numpy as jnp
from jax import lax
from jax.sharding import PartitionSpec as P


def extended_2(block, sides, width):
    for axis, dim in sides:
        count = lax.axis_size(axis)
        forward = [(i, i + 1) for i in range(count - 1)]
        forward.append((count - 1, 0))
        backward = [(target, source) for source, target in forward]
        low = lax.ppermute(
            lax.slice_in_dim(block, block.shape[dim] - width, None, axis=dim), axis, forward
        )
        high = lax.ppermute(lax.slice_in_dim(block, 0, width, axis=dim), axis, backward)
        block = jnp.concatenate([low, block, high], axis=dim)
    return block


def conv_local(extended, weight):
    out_width = extended.shape[2] - 2
    lat_rows = extended.shape[3]
    padded = jnp.pad(extended, ((0, 0), (0, 0), (0, 0), (1, 1)))
    summed = jnp.zeros((extended.shape[0], weight.shape[2], out_width, lat_rows), jnp.float32)
    for row_tap in range(3):
        for col_tap in range(3):
            window = padded[:, :, row_tap : row_tap + out_width, col_tap : col_tap + lat_rows]
            summed = summed + jnp.einsum(
                "oc,pcxy->poxy",
                weight[row_tap, col_tap],
                window,
                preferred_element_type=jnp.float32,
            )
    return summed


def denoise_local(states, observed, obs_weight, w_in, w_mid, w_out):
    extended = extended_2(states, (("lon", 2),), 1)
    first_act = jax.nn.silu(conv_local(extended, w_in)).astype(jnp.bfloat16)
    first_ext = extended_2(first_act, (("lon", 2),), 1)
    second_act = jax.nn.silu(conv_local(first_ext, w_mid)).astype(jnp.bfloat16)
    second_ext = extended_2(second_act, (("lon", 2),), 1)
    noise_pred = conv_local(second_ext, w_out)
    current = states.astype(jnp.float32)
    updated = (
        current
        - 0.5 * noise_pred
        + 0.25 * obs_weight[None, None] * (observed.astype(jnp.float32)[None] - current)
    )
    return updated.astype(jnp.bfloat16)


def continue_slots(slabs, slot_ancestors):
    slab_piece = lax.all_gather(slabs, "dom", axis=0, tiled=True)
    piece_rows = slab_piece.shape[0]
    inside = (slot_ancestors >= 0) & (slot_ancestors < piece_rows)
    chosen = jnp.take(slab_piece, jnp.clip(slot_ancestors, 0, piece_rows - 1), axis=0)
    return jnp.where(inside[:, None, None, None], chosen, jnp.zeros_like(slabs))


def on_device(particles, observed, precision, stations, ancestors, tempering, w_in, w_mid, w_out):
    obs_weight = stations.astype(jnp.float32) * precision
    misfit_cell = particles.astype(jnp.float32) - observed.astype(jnp.float32)[None]
    local_sums = jnp.sum(obs_weight[None, None] * misfit_cell * misfit_cell, axis=(1, 2, 3))
    band_sums = lax.psum(local_sums, "lon")
    every_sum = lax.all_gather(band_sums, "dom", axis=0, tiled=True)
    center = jnp.mean(every_sum)
    deviation = every_sum - center
    spread = jnp.sqrt(jnp.mean(deviation * deviation) + 1.0)
    log_weights = -0.5 * tempering[0] * deviation / spread
    expo = jnp.exp(log_weights)
    weights_all = expo / jnp.sum(expo)
    slot_count = ancestors.shape[0]
    own_weights = lax.dynamic_slice_in_dim(
        weights_all, lax.axis_index("dom") * slot_count, slot_count
    )
    continued = continue_slots(particles, ancestors)
    new_particles = denoise_local(continued, observed, obs_weight, w_in, w_mid, w_out)
    return (new_particles, own_weights)


def solution(mesh):
    return jax.shard_map(
        on_device,
        mesh=mesh,
        in_specs=(
            P(("ens", "dom"), None, "lon", None),
            P("ens", "lon", None),
            P(("ens", "lon"), None),
            P(("ens", "lon"), None),
            P(("ens", "dom")),
            P("ens"),
            P(),
            P(),
            P(),
        ),
        out_specs=(P(("ens", "dom"), None, "lon", None), P(("ens", "dom"))),
        check_vma=False,
    )
```

profile of v0, /device:TPU:0, one launch (start us, length us, event | category | flops | bytes accessed | tf_op | source)
XLA Modules:
  0.0 159.0 jit_solution(17750243368687318687)
XLA Ops:
  7.2 0.7 all-gather.2.cloned.1.call-update
  8.0 1.3 copy.19
  9.3 0.9 fusion.5
  10.2 13.4 %psum.7 = f32[2]{0:T(128)S(1)} all-reduce(f32[2]{0:T(128)S(1)} %fusion.5), channel_id=1, replica_groups=mesh['ens'=2,'lon'=4,'dom'=4] {'lon'}, use_global_device_ids=true, to_apply=%region_1.0 | all-reduce | flops 2 | bytes 16 | tf_op jit(solution)/shard_map/psum | solution.py:66
  23.7 0.6 dynamic-slice
  25.1 6.1 %all-reduce.3 = f32[8]{0:T(128)S(1)} all-reduce(f32[8]{0:T(128)S(1)} %dynamic-update-slice), channel_id=1, replica_groups=mesh['ens'=2,'lon'=4,'dom'=4] {'dom'}, use_global_device_ids=true, to_apply=%add.3 | all-reduce | flops 8 | bytes 64
  31.9 0.6 reduce_sum.37
  33.2 0.6 multiply_reduce_fusion
  34.5 0.6 fusion.151
  35.1 0.6 broadcast_divide_fusion
  35.8 0.6 dynamic_slice.3
  36.4 25.2 %all-gather.2.cloned.1.call-done = bf16[8,69,24,256]{3,2,1,0:T(8,128)(2,1)} async-done(((bf16[2,69,24,256]{3,2,1,0:T(8,128)(2,1)}), bf16[8,69,24,256]{3,2,1,0:T(8,128)(2,1)}) %all-gather.2.cloned.1.call-update) | async-done | bytes 6782992 | tf_op jit(solution)/shard_map/all_gather | solution.py:55
  61.6 3.6 %gather_fusion = bf16[2,69,24,256]{3,2,1,0:T(8,128)(2,1)S(1)} fusion(bf16[8,69,24,256]{3,2,1,0:T(8,128)(2,1)} %all-gather.2.cloned.1.call-done, s32[1024]{0:T(1024)S(1)} %pad_clamp_fusion), kind=kCustom, calls=%fused_computation | custom fusion | bytes 3391496 | tf_op jit(solution)/shard_map/jit(_take)/gather | solution.py:58
  65.7 1.5 collective-permute-start
  67.2 2.3 %collective-permute-start.1 = (bf16[2,69,1,256]{3,1,2,0:T(8,128)(2,1)S(1)}, bf16[2,69,1,256]{3,1,2,0:T(8,128)(2,1)S(1)}, u32[]{:S(2)}, u32[]{:S(2)}) collective-permute-start(bf16[2,69,1,256]{3,1,2,0:T(8,128)(2,1)S(1)} %get-tuple-element.15), channel_id=1, source_target_pairs={{4,0},{8,4},{12,8},{0,12},{5,1},{9,5},{13,9},{1,13},{6,2},{10,6},{... | collective-permute-start | bytes 211976 | tf_op jit(solution)/shard_map/ppermute | solution.py:16
  69.6 2.6 %fusion.111 = f32[2,24,256,64]{2,3,1,0:T(8,128)} fusion(bf16[3,3,64,69]{3,2,1,0:T(8,128)(2,1)S(1)} %copy-done.3, bf16[2,69,24,256]{3,2,1,0:T(8,128)(2,1)S(1)} %gather_fusion, pred[2]{0:T(512)(128)(4,1)S(1)} %get-tuple-element.12, pred[2]{0:T(512)(128)(4,1)S(1)} %get-tuple-element.20), kind=kOutput, calls=%fused_computation.123 | convolution fusion | flops 110223360 | bytes 4858880 | tf_op jit(solution)/shard_map/oc,pcxy->poxy/dot_general | solution.py:29
  72.4 0.6 collective-permute-done.1
  73.0 2.0 %fusion.18 = bf16[2,69,26,258]{3,1,2,0:T(8,128)(2,1)S(1)} fusion(bf16[2,69,1,256]{3,1,2,0:T(8,128)(2,1)S(1)} %collective-permute-done.1, bf16[2,69,24,256]{3,1,2,0:T(8,128)(2,1)S(1)} %fusion.44, bf16[2,69,1,256]{3,1,2,0:T(8,128)(2,1)S(1)} %collective-permute-done), kind=kLoop, calls=%fused_computation.30 | loop fusion | flops 11108448 | bytes 3688464 | tf_op jit(solution)/shard_map/concatenate | solution.py:17
  75.6 0.8 fusion.36
  77.0 0.8 fusion.40
  77.8 2.2 %fusion.42 = f32[2,24,256,64]{2,3,1,0:T(8,128)} fusion(bf16[2,69,26,258]{3,1,2,0:T(8,128)(2,1)S(1)} %fusion.18, bf16[3,3,64,69]{3,2,1,0:T(8,128)(2,1)S(1)} %copy-done.3), kind=kOutput, calls=%fused_computation.56 | convolution fusion | flops 108527616 | bytes 4931584 | tf_op jit(solution)/shard_map/oc,pcxy->poxy/dot_general | solution.py:29
  80.0 2.2 %fusion.24 = f32[2,24,256,64]{2,3,1,0:T(8,128)} fusion(bf16[2,69,24,256]{3,1,2,0:T(8,128)(2,1)S(1)} %fusion.44, bf16[2,69,1,256]{3,1,2,0:T(8,128)(2,1)S(1)} %collective-permute-done, bf16[3,3,64,69]{3,2,1,0:T(8,128)(2,1)S(1)} %copy-done.3), kind=kOutput, calls=%fused_computation.38 | convolution fusion | flops 112060416 | bytes 5005312 | tf_op jit(solution)/shard_map/oc,pcxy->poxy/dot_general | solution.py:29
  82.2 2.2 %fusion.28 = f32[2,24,256,64]{2,3,1,0:T(8,128)} fusion(bf16[2,69,1,256]{3,1,2,0:T(8,128)(2,1)S(1)} %collective-permute-done.1, bf16[2,69,24,256]{3,1,2,0:T(8,128)(2,1)S(1)} %fusion.44, bf16[3,3,64,69]{3,2,1,0:T(8,128)(2,1)S(1)} %copy-done.3), kind=kOutput, calls=%fused_computation.42 | convolution fusion | flops 112060416 | bytes 5005312 | tf_op jit(solution)/shard_map/oc,pcxy->poxy/dot_general | solution.py:29
  84.4 6.0 %fusion.15 = bf16[2,64,24,256]{3,1,2,0:T(8,128)(2,1)S(1)} fusion(f32[2,24,256,64]{2,3,1,0:T(8,128)} %fusion.28, f32[2,24,256,64]{2,3,1,0:T(8,128)S(1)} %fusion.34, f32[2,24,256,64]{2,3,1,0:T(8,128)S(1)} %fusion.36, f32[2,24,256,64]{2,3,1,0:T(8,128)} %fusion.111, f32[2,24,256,64]{2,3,1,0:T(8,128)S(1)} %fusion.38, f32[2,24,256,64]{2,3,1,0:T(8,128)S(1)} %fusion.40, ...), kind=kOutput, calls=%fused_computation.27 | convolution fusion | flops 118751232 | bytes 28524544 | tf_op jit(solution)/shard_map/oc,pcxy->poxy/dot_general | solution.py:29
  90.4 1.2 collective-permute-start.2
  91.6 2.7 %collective-permute-start.3 = (bf16[2,64,1,256]{3,1,2,0:T(8,128)(2,1)S(1)}, bf16[2,64,1,256]{3,1,2,0:T(8,128)(2,1)S(1)}, u32[]{:S(2)}, u32[]{:S(2)}) collective-permute-start(bf16[2,64,1,256]{3,1,2,0:T(8,128)(2,1)S(1)} %get-tuple-element.19), channel_id=1, source_target_pairs={{4,0},{8,4},{12,8},{0,12},{5,1},{9,5},{13,9},{1,13},{6,2},{10,6},{... | collective-permute-start | bytes 196616 | tf_op jit(solution)/shard_map/ppermute | solution.py:16
  94.9 1.8 %collective-permute-done.2 = bf16[2,64,1,256]{3,1,2,0:T(8,128)(2,1)S(1)} collective-permute-done((bf16[2,64,1,256]{3,1,2,0:T(8,128)(2,1)S(1)}, bf16[2,64,1,256]{3,1,2,0:T(8,128)(2,1)S(1)}, u32[]{:S(2)}, u32[]{:S(2)}) %collective-permute-start.2) | collective-permute-done | bytes 65568 | tf_op jit(solution)/shard_map/ppermute | solution.py:13
  96.8 1.8 %fusion.23 = bf16[2,64,26,258]{3,1,2,0:T(8,128)(2,1)S(1)} fusion(bf16[2,64,1,256]{3,1,2,0:T(8,128)(2,1)S(1)} %collective-permute-done.3, bf16[2,64,24,256]{3,1,2,0:T(8,128)(2,1)S(1)} %fusion.15, bf16[2,64,1,256]{3,1,2,0:T(8,128)(2,1)S(1)} %collective-permute-done.2), kind=kLoop, calls=%fused_computation.37 | loop fusion | flops 10303488 | bytes 3421184 | tf_op jit(solution)/shard_map/concatenate | solution.py:17
  99.1 0.7 fusion.77
  100.4 2.3 %fusion.81 = f32[2,24,256,64]{2,3,1,0:T(8,128)} fusion(bf16[2,64,26,258]{3,1,2,0:T(8,128)(2,1)S(1)} %fusion.23, bf16[3,3,64,64]{3,2,1,0:T(8,128)(2,1)S(1)} %copy-done.1), kind=kOutput, calls=%fused_computation.91 | convolution fusion | flops 100663296 | bytes 4734976 | tf_op jit(solution)/shard_map/oc,pcxy->poxy/dot_general | solution.py:29
  102.7 2.2 %fusion.85 = f32[2,24,256,64]{2,3,1,0:T(8,128)} fusion(bf16[2,64,26,258]{3,1,2,0:T(8,128)(2,1)S(1)} %fusion.23, bf16[3,3,64,64]{3,2,1,0:T(8,128)(2,1)S(1)} %copy-done.1), kind=kOutput, calls=%fused_computation.96 | convolution fusion | flops 100663296 | bytes 4734976 | tf_op jit(solution)/shard_map/oc,pcxy->poxy/dot_general | solution.py:29
  104.9 2.2 %fusion.83 = f32[2,24,256,64]{2,3,1,0:T(8,128)} fusion(bf16[2,64,24,256]{3,1,2,0:T(8,128)(2,1)S(1)} %fusion.15, bf16[2,64,1,256]{3,1,2,0:T(8,128)(2,1)S(1)} %collective-permute-done.2, bf16[3,3,64,64]{3,2,1,0:T(8,128)(2,1)S(1)} %copy-done.1), kind=kOutput, calls=%fused_computation.94 | convolution fusion | flops 103809024 | bytes 4800512 | tf_op jit(solution)/shard_map/oc,pcxy->poxy/dot_general | solution.py:29
  107.1 2.2 %fusion.73 = f32[2,24,256,64]{2,3,1,0:T(8,128)} fusion(bf16[2,64,1,256]{3,1,2,0:T(8,128)(2,1)S(1)} %collective-permute-done.3, bf16[2,64,24,256]{3,1,2,0:T(8,128)(2,1)S(1)} %fusion.15, bf16[3,3,64,64]{3,2,1,0:T(8,128)(2,1)S(1)} %copy-done.1), kind=kOutput, calls=%fused_computation.83 | convolution fusion | flops 103809024 | bytes 4800512 | tf_op jit(solution)/shard_map/oc,pcxy->poxy/dot_general | solution.py:29
  109.3 5.9 %fusion.16 = bf16[2,64,24,256]{3,1,2,0:T(8,128)(2,1)S(1)} fusion(f32[2,24,256,64]{2,3,1,0:T(8,128)} %fusion.73, f32[2,24,256,64]{2,3,1,0:T(8,128)S(1)} %fusion.75, f32[2,24,256,64]{2,3,1,0:T(8,128)S(1)} %fusion.77, f32[2,24,256,64]{2,3,1,0:T(8,128)S(1)} %fusion.101, f32[2,24,256,64]{2,3,1,0:T(8,128)S(1)} %fusion.79, f32[2,24,256,64]{2,3,1,0:T(8,128)} %fusion.81, ...), kind=kOutput, calls=%fused_computation.28 | convolution fusion | flops 110886912 | bytes 28327936 | tf_op jit(solution)/shard_map/oc,pcxy->poxy/dot_general | solution.py:29
  115.3 0.6 collective-permute-start.4
  115.9 3.3 %collective-permute-start.5 = (bf16[2,64,1,256]{3,1,2,0:T(8,128)(2,1)S(1)}, bf16[2,64,1,256]{3,1,2,0:T(8,128)(2,1)S(1)}, u32[]{:S(2)}, u32[]{:S(2)}) collective-permute-start(bf16[2,64,1,256]{3,1,2,0:T(8,128)(2,1)S(1)} %get-tuple-element.17), channel_id=1, source_target_pairs={{4,0},{8,4},{12,8},{0,12},{5,1},{9,5},{13,9},{1,13},{6,2},{10,6},{... | collective-permute-start | bytes 196616 | tf_op jit(solution)/shard_map/ppermute | solution.py:16
  119.2 0.7 fusion.91
  119.9 1.6 collective-permute-done.4
  121.4 1.8 %select_maximum_fusion = bf16[2,64,26,258]{3,1,2,0:T(8,128)(2,1)S(1)} fusion(bf16[2,64,1,256]{3,1,2,0:T(8,128)(2,1)S(1)} %collective-permute-done.5, bf16[2,64,24,256]{3,1,2,0:T(8,128)(2,1)S(1)} %fusion.16, bf16[2,64,1,256]{3,1,2,0:T(8,128)(2,1)S(1)} %collective-permute-done.4), kind=kLoop, calls=%fused_computation.31 | loop fusion | flops 10303488 | bytes 3421184 | tf_op jit(solution)/shard_map/concatenate | solution.py:17
  123.2 2.5 %fusion.59 = f32[2,24,256,69]{2,3,1,0:T(8,128)} fusion(bf16[2,64,26,258]{3,1,2,0:T(8,128)(2,1)S(1)} %select_maximum_fusion, bf16[3,3,69,64]{2,3,1,0:T(8,128)(2,1)S(1)} %copy-done.2), kind=kOutput, calls=%fused_computation.70 | convolution fusion | flops 108527616 | bytes 4980736 | tf_op jit(solution)/shard_map/oc,pcxy->poxy/dot_general | solution.py:29
  125.7 2.6 %fusion.61 = f32[2,24,256,69]{2,3,1,0:T(8,128)} fusion(bf16[2,64,26,258]{3,1,2,0:T(8,128)(2,1)S(1)} %select_maximum_fusion, bf16[3,3,69,64]{2,3,1,0:T(8,128)(2,1)S(1)} %copy-done.2), kind=kOutput, calls=%fused_computation.72 | convolution fusion | flops 108527616 | bytes 4980736 | tf_op jit(solution)/shard_map/oc,pcxy->poxy/dot_general | solution.py:29
  128.2 2.5 %fusion.63 = f32[2,24,256,69]{2,3,1,0:T(8,128)} fusion(bf16[2,64,26,258]{3,1,2,0:T(8,128)(2,1)S(1)} %select_maximum_fusion, bf16[3,3,69,64]{2,3,1,0:T(8,128)(2,1)S(1)} %copy-done.2), kind=kOutput, calls=%fused_computation.74 | convolution fusion | flops 108527616 | bytes 4980736 | tf_op jit(solution)/shard_map/oc,pcxy->poxy/dot_general | solution.py:29
  130.8 2.5 %fusion.65 = f32[2,24,256,69]{2,3,1,0:T(8,128)} fusion(bf16[2,64,26,258]{3,1,2,0:T(8,128)(2,1)S(1)} %select_maximum_fusion, bf16[3,3,69,64]{2,3,1,0:T(8,128)(2,1)S(1)} %copy-done.2), kind=kOutput, calls=%fused_computation.76 | convolution fusion | flops 108527616 | bytes 4980736 | tf_op jit(solution)/shard_map/oc,pcxy->poxy/dot_general | solution.py:29
  133.3 2.4 %fusion.67 = f32[2,24,256,69]{2,3,1,0:T(8,128)} fusion(bf16[2,64,26,258]{3,1,2,0:T(8,128)(2,1)S(1)} %select_maximum_fusion, bf16[3,3,69,64]{2,3,1,0:T(8,128)(2,1)S(1)} %copy-done.2), kind=kOutput, calls=%fused_computation.78 | convolution fusion | flops 108527616 | bytes 4980736 | tf_op jit(solution)/shard_map/oc,pcxy->poxy/dot_general | solution.py:29
  135.7 2.4 %fusion.47 = f32[2,24,256,69]{2,3,1,0:T(8,128)} fusion(bf16[2,64,24,256]{3,1,2,0:T(8,128)(2,1)S(1)} %fusion.16, bf16[2,64,1,256]{3,1,2,0:T(8,128)(2,1)S(1)} %collective-permute-done.4, bf16[3,3,69,64]{2,3,1,0:T(8,128)(2,1)S(1)} %copy-done.2), kind=kOutput, calls=%fused_computation.60 | convolution fusion | flops 111804416 | bytes 5046272 | tf_op jit(solution)/shard_map/oc,pcxy->poxy/dot_general | solution.py:29
  138.1 2.4 %fusion.51 = f32[2,24,256,69]{2,3,1,0:T(8,128)} fusion(bf16[2,64,1,256]{3,1,2,0:T(8,128)(2,1)S(1)} %collective-permute-done.5, bf16[2,64,24,256]{3,1,2,0:T(8,128)(2,1)S(1)} %fusion.16, bf16[3,3,69,64]{2,3,1,0:T(8,128)(2,1)S(1)} %copy-done.2), kind=kOutput, calls=%fused_computation.64 | convolution fusion | flops 111804416 | bytes 5046272 | tf_op jit(solution)/shard_map/oc,pcxy->poxy/dot_general | solution.py:29
  140.5 10.1 %fusion.3 = bf16[2,69,24,256]{3,1,2,0:T(8,128)(2,1)S(1)} fusion(f32[2,24,256,69]{2,3,1,0:T(8,128)} %fusion.51, f32[2,24,256,69]{2,3,1,0:T(8,128)} %fusion.59, f32[2,24,256,69]{2,3,1,0:T(8,128)} %fusion.61, f32[2,24,256,69]{2,3,1,0:T(8,128)S(1)} %fusion.91, f32[2,24,256,69]{2,3,1,0:T(8,128)} %fusion.63, f32[2,24,256,69]{2,3,1,0:T(8,128)} %fusion.65, ...), kind=kOutput, calls=%fused_computation.11 | convolution fusion | flops 122941440 | bytes 34055168 | tf_op jit(solution)/shard_map/oc,pcxy->poxy/dot_general | solution.py:29
  150.6 1.5 copy.21
  (34 shorter events, 3.9 us)
Async XLA Ops:
  7.2 2.2 %copy-start = (bf16[2,69,24,256]{3,2,1,0:T(8,128)(2,1)S(1)}, bf16[2,69,24,256]{3,2,1,0:T(8,128)(2,1)}, u32[]{:S(2)}) copy-start(bf16[2,69,24,256]{3,2,1,0:T(8,128)(2,1)} %param.9) | copy-start | bytes 5087236
  7.2 2.1 %copy-start.5 = (s32[24,256]{1,0:T(8,128)S(1)}, s32[24,256]{1,0:T(8,128)}, u32[]{:S(2)}) copy-start(s32[24,256]{1,0:T(8,128)} %param.12) | copy-start | bytes 73732
  7.2 2.1 %copy-start.4 = (f32[24,256]{1,0:T(8,128)S(1)}, f32[24,256]{1,0:T(8,128)}, u32[]{:S(2)}) copy-start(f32[24,256]{1,0:T(8,128)} %param.11) | copy-start | bytes 73732
  7.2 54.4 %all-gather.2.cloned.1.call-start = ((), (), s32[]{:S(2)}) async-start(), calls=%async_computation | async-start | bytes 8478720 | tf_op jit(solution)/shard_map/all_gather | solution.py:55
  7.9 15.7 %copy-start.7 = (u32[32]{0:T(128)S(1)}, u32[32]{0:T(128)}, u32[]{:S(2)}) copy-start(u32[32]{0:T(128)} %constant.60) | copy-start | bytes 388
  7.9 28.4 %copy-start.6 = (s32[2]{0:T(128)S(1)}, s32[2]{0:T(128)}, u32[]{:S(2)}) copy-start(s32[2]{0:T(128)} %param.13) | copy-start | bytes 28
  65.2 4.4 %copy-start.3 = (bf16[3,3,64,69]{3,2,1,0:T(8,128)(2,1)S(1)}, bf16[3,3,64,69]{3,2,1,0:T(8,128)(2,1)}, u32[]{:S(2)}) copy-start(bf16[3,3,64,69]{3,2,1,0:T(8,128)(2,1)} %param.15) | copy-start | bytes 238468
  65.7 6.7 %collective-permute-start = (bf16[2,69,1,256]{3,1,2,0:T(8,128)(2,1)S(1)}, bf16[2,69,1,256]{3,1,2,0:T(8,128)(2,1)S(1)}, u32[]{:S(2)}, u32[]{:S(2)}) collective-permute-start(bf16[2,69,1,256]{3,1,2,0:T(8,128)(2,1)S(1)} %get-tuple-element.14), channel_id=1, source_target_pairs={{0,4},{4,8},{8,12},{12,0},{1,5},{5,9},{9,13},{13,1},{2,6},{6,10},{... | collective-permute-start | bytes 211976 | tf_op jit(solution)/shard_map/ppermute | solution.py:13
  67.2 5.7 %collective-permute-start.1 = (bf16[2,69,1,256]{3,1,2,0:T(8,128)(2,1)S(1)}, bf16[2,69,1,256]{3,1,2,0:T(8,128)(2,1)S(1)}, u32[]{:S(2)}, u32[]{:S(2)}) collective-permute-start(bf16[2,69,1,256]{3,1,2,0:T(8,128)(2,1)S(1)} %get-tuple-element.15), channel_id=1, source_target_pairs={{4,0},{8,4},{12,8},{0,12},{5,1},{9,5},{13,9},{1,13},{6,2},{10,6},{... | collective-permute-start | bytes 211976 | tf_op jit(solution)/shard_map/ppermute | solution.py:16
  84.4 9.9 %copy-start.1 = (bf16[3,3,64,64]{3,2,1,0:T(8,128)(2,1)S(1)}, bf16[3,3,64,64]{3,2,1,0:T(8,128)(2,1)}, u32[]{:S(2)}) copy-start(bf16[3,3,64,64]{3,2,1,0:T(8,128)(2,1)} %param.16) | copy-start | bytes 221188
  90.4 6.3 %collective-permute-start.2 = (bf16[2,64,1,256]{3,1,2,0:T(8,128)(2,1)S(1)}, bf16[2,64,1,256]{3,1,2,0:T(8,128)(2,1)S(1)}, u32[]{:S(2)}, u32[]{:S(2)}) collective-permute-start(bf16[2,64,1,256]{3,1,2,0:T(8,128)(2,1)S(1)} %get-tuple-element.18), channel_id=1, source_target_pairs={{0,4},{4,8},{8,12},{12,0},{1,5},{5,9},{9,13},{13,1},{2,6},{6,10},{... | collective-permute-start | bytes 196616 | tf_op jit(solution)/shard_map/ppermute | solution.py:13
  91.6 5.2 %collective-permute-start.3 = (bf16[2,64,1,256]{3,1,2,0:T(8,128)(2,1)S(1)}, bf16[2,64,1,256]{3,1,2,0:T(8,128)(2,1)S(1)}, u32[]{:S(2)}, u32[]{:S(2)}) collective-permute-start(bf16[2,64,1,256]{3,1,2,0:T(8,128)(2,1)S(1)} %get-tuple-element.19), channel_id=1, source_target_pairs={{4,0},{8,4},{12,8},{0,12},{5,1},{9,5},{13,9},{1,13},{6,2},{10,6},{... | collective-permute-start | bytes 196616 | tf_op jit(solution)/shard_map/ppermute | solution.py:16
  109.3 9.9 %copy-start.2 = (bf16[3,3,69,64]{2,3,1,0:T(8,128)(2,1)S(1)}, bf16[3,3,69,64]{2,3,1,0:T(8,128)(2,1)}, u32[]{:S(2)}) copy-start(bf16[3,3,69,64]{2,3,1,0:T(8,128)(2,1)} %param.17) | copy-start | bytes 238468
  115.3 6.2 %collective-permute-start.4 = (bf16[2,64,1,256]{3,1,2,0:T(8,128)(2,1)S(1)}, bf16[2,64,1,256]{3,1,2,0:T(8,128)(2,1)S(1)}, u32[]{:S(2)}, u32[]{:S(2)}) collective-permute-start(bf16[2,64,1,256]{3,1,2,0:T(8,128)(2,1)S(1)} %get-tuple-element.16), channel_id=1, source_target_pairs={{0,4},{4,8},{8,12},{12,0},{1,5},{5,9},{9,13},{13,1},{2,6},{6,10},{... | collective-permute-start | bytes 196616 | tf_op jit(solution)/shard_map/ppermute | solution.py:13
  115.9 5.6 %collective-permute-start.5 = (bf16[2,64,1,256]{3,1,2,0:T(8,128)(2,1)S(1)}, bf16[2,64,1,256]{3,1,2,0:T(8,128)(2,1)S(1)}, u32[]{:S(2)}, u32[]{:S(2)}) collective-permute-start(bf16[2,64,1,256]{3,1,2,0:T(8,128)(2,1)S(1)} %get-tuple-element.17), channel_id=1, source_target_pairs={{4,0},{8,4},{12,8},{0,12},{5,1},{9,5},{13,9},{1,13},{6,2},{10,6},{... | collective-permute-start | bytes 196616 | tf_op jit(solution)/shard_map/ppermute | solution.py:16
Sparse Core Ops, SparseCore 0:
  9.6 51.9 all-gather.1
where the time goes:
time: 159 us
  matrix products  63.2 us (40%)
  waiting for transfers between devices  30.2 us (19%)
  blocking collectives  19.6 us (12%)
  between operations  16.9 us (11%)
  starting transfers between devices  11.7 us (7%)
  other arithmetic  9.41 us (6%)
  local copies, waits for them, and re-layouts  7.92 us (5%)
    dot_general x27, matrix products, conv_local(): jnp.einsum('oc,pcxy->poxy', weight[row_tap, col_tap], window, preferred_e...  63.2 us
    all_gather x1, waiting for transfers between devices, continue_slots(): slab_piece = lax.all_gather(slabs, 'dom', axis=0, tiled=True)  25.2 us
    psum x1, blocking collectives, on_device(): band_sums = lax.psum(local_sums, 'lon')  13.4 us
    ppermute x3, starting transfers between devices, extended_2(): lax.ppermute(lax.slice_in_dim(block, 0, width, axis=dim), axis, backward)  8.36 us
    unnamed x1, blocking collectives  6.14 us
    concatenate x3, other arithmetic, extended_2(): block = jnp.concatenate([low, block, high], axis=dim)  5.59 us
    ppermute x3, waiting for transfers between devices, extended_2(): lax.ppermute(lax.slice_in_dim(block, block.shape[dim] - width, None, axis...  3.61 us
    gather x1, local copies, waits for them, and re-layouts, continue_slots(): jnp.take(slab_piece, jnp.clip(slot_ancestors, 0, piece_rows - 1), axis=0)  3.58 us
  transfers between devices with their start and end apart: 7, of which 6 were waited for; matrix products, arithmetic and copies ran while one was open for 6% of the time, Pallas kernels for 0%

commit v1 on v0

--- a/solution.py
+++ b/solution.py
@@ -2,6 +2,11 @@
 import jax.numpy as jnp
 from jax import lax
 from jax.sharding import PartitionSpec as P
+
+
+def gather_and_add(x, axis):
+    pieces = lax.all_gather(x, axis)
+    return jnp.sum(pieces, axis=0)
 
 
 def extended_2(block, sides, width):
@@ -63,7 +68,7 @@
     obs_weight = stations.astype(jnp.float32) * precision
     misfit_cell = particles.astype(jnp.float32) - observed.astype(jnp.float32)[None]
     local_sums = jnp.sum(obs_weight[None, None] * misfit_cell * misfit_cell, axis=(1, 2, 3))
-    band_sums = lax.psum(local_sums, "lon")
+    band_sums = gather_and_add(local_sums, "lon")
     every_sum = lax.all_gather(band_sums, "dom", axis=0, tiled=True)
     center = jnp.mean(every_sum)
     deviation = every_sum - center

time: 159 us -> 159 us (level)
    psum x1 -> x0, blocking collectives: 13.4 us -> none  [on_device(): band_sums = lax.psum(local_sums, 'lon')]
    unnamed x1 -> x2, blocking collectives: 6.14 us -> 19.6 us
  transfers between devices with their start and end apart: 7 -> 7, of which waited for: 6 -> 6; matrix products, arithmetic and copies ran while one was open for 6% -> 7% of each run, Pallas kernels for 0% -> 0%
where the time goes in v1:
time: 159 us
  matrix products  63.2 us (40%)
  waiting for transfers between devices  28.7 us (18%)
  blocking collectives  19.6 us (12%)
  between operations  17.6 us (11%)
  starting transfers between devices  11.7 us (7%)
  other arithmetic  9.43 us (6%)
  local copies, waits for them, and re-layouts  8.78 us (6%)
    dot_general x27, matrix products, conv_local(): jnp.einsum('oc,pcxy->poxy', weight[row_tap, col_tap], window, preferred_e...  63.2 us
    all_gather x1, waiting for transfers between devices, continue_slots(): slab_piece = lax.all_gather(slabs, 'dom', axis=0, tiled=True)  23.7 us
    unnamed x2, blocking collectives  19.6 us
    ppermute x3, starting transfers between devices, extended_2(): lax.ppermute(lax.slice_in_dim(block, 0, width, axis=dim), axis, backward)  8.37 us
    concatenate x3, other arithmetic, extended_2(): block = jnp.concatenate([low, block, high], axis=dim)  5.59 us
    ppermute x3, waiting for transfers between devices, extended_2(): lax.ppermute(lax.slice_in_dim(block, block.shape[dim] - width, None, axis...  3.64 us
    gather x1, local copies, waits for them, and re-layouts, continue_slots(): jnp.take(slab_piece, jnp.clip(slot_ancestors, 0, piece_rows - 1), axis=0)  3.58 us
    ppermute x3, starting transfers between devices, extended_2(): lax.ppermute(lax.slice_in_dim(block, block.shape[dim] - width, None, axis...  3.3 us
  transfers between devices with their start and end apart: 7, of which 6 were waited for; matrix products, arithmetic and copies ran while one was open for 7% of the time, Pallas kernels for 0%

profile of v1, /device:TPU:0, one launch (start us, length us, event | category | flops | bytes accessed | tf_op | source)
XLA Modules:
  0.0 159.0 jit_solution(16034325286232587705)
XLA Ops:
  7.3 0.7 all-gather.3.cloned.1.call-update
  8.0 1.3 copy.19
  9.3 0.6 dynamic-slice
  10.6 0.9 fusion.5
  11.7 13.4 %all-reduce.3 = f32[8]{0:T(128)S(1)} all-reduce(f32[8]{0:T(128)S(1)} %dynamic-update-slice), channel_id=2, replica_groups=mesh['ens'=2,'lon'=4,'dom'=4] {'lon'}, use_global_device_ids=true, to_apply=%add.3 | all-reduce | flops 8 | bytes 64
  25.1 0.6 dynamic-slice.1
  26.7 6.1 %all-reduce.4 = f32[8]{0:T(128)S(1)} all-reduce(f32[8]{0:T(128)S(1)} %dynamic-update-slice.1), channel_id=1, replica_groups=mesh['ens'=2,'lon'=4,'dom'=4] {'dom'}, use_global_device_ids=true, to_apply=%add.4 | all-reduce | flops 8 | bytes 64
  33.5 0.6 reduce_sum.47
  34.7 0.6 multiply_reduce_fusion
  36.0 0.6 fusion.151
  36.7 0.6 broadcast_divide_fusion
  37.3 0.6 dynamic_slice.3
  37.9 23.7 %all-gather.3.cloned.1.call-done = bf16[8,69,24,256]{3,2,1,0:T(8,128)(2,1)} async-done(((bf16[2,69,24,256]{3,2,1,0:T(8,128)(2,1)}), bf16[8,69,24,256]{3,2,1,0:T(8,128)(2,1)}) %all-gather.3.cloned.1.call-update) | async-done | bytes 6782992 | tf_op jit(solution)/shard_map/all_gather | solution.py:60
  61.6 3.6 %gather_fusion = bf16[2,69,24,256]{3,2,1,0:T(8,128)(2,1)S(1)} fusion(bf16[8,69,24,256]{3,2,1,0:T(8,128)(2,1)} %all-gather.3.cloned.1.call-done, s32[1024]{0:T(1024)S(1)} %pad_clamp_fusion), kind=kCustom, calls=%fused_computation | custom fusion | bytes 3391496 | tf_op jit(solution)/shard_map/jit(_take)/gather | solution.py:63
  65.7 1.5 collective-permute-start
  67.2 2.3 %collective-permute-start.1 = (bf16[2,69,1,256]{3,1,2,0:T(8,128)(2,1)S(1)}, bf16[2,69,1,256]{3,1,2,0:T(8,128)(2,1)S(1)}, u32[]{:S(2)}, u32[]{:S(2)}) collective-permute-start(bf16[2,69,1,256]{3,1,2,0:T(8,128)(2,1)S(1)} %get-tuple-element.15), channel_id=1, source_target_pairs={{4,0},{8,4},{12,8},{0,12},{5,1},{9,5},{13,9},{1,13},{6,2},{10,6},{... | collective-permute-start | bytes 211976 | tf_op jit(solution)/shard_map/ppermute | solution.py:21
  69.6 2.6 %fusion.111 = f32[2,24,256,64]{2,3,1,0:T(8,128)} fusion(bf16[3,3,64,69]{3,2,1,0:T(8,128)(2,1)S(1)} %copy-done.3, bf16[2,69,24,256]{3,2,1,0:T(8,128)(2,1)S(1)} %gather_fusion, pred[2]{0:T(512)(128)(4,1)S(1)} %get-tuple-element.12, pred[2]{0:T(512)(128)(4,1)S(1)} %get-tuple-element.20), kind=kOutput, calls=%fused_computation.123 | convolution fusion | flops 110223360 | bytes 4858880 | tf_op jit(solution)/shard_map/oc,pcxy->poxy/dot_general | solution.py:34
  72.4 0.6 collective-permute-done.1
  73.0 2.0 %fusion.18 = bf16[2,69,26,258]{3,1,2,0:T(8,128)(2,1)S(1)} fusion(bf16[2,69,1,256]{3,1,2,0:T(8,128)(2,1)S(1)} %collective-permute-done.1, bf16[2,69,24,256]{3,1,2,0:T(8,128)(2,1)S(1)} %fusion.44, bf16[2,69,1,256]{3,1,2,0:T(8,128)(2,1)S(1)} %collective-permute-done), kind=kLoop, calls=%fused_computation.30 | loop fusion | flops 11108448 | bytes 3688464 | tf_op jit(solution)/shard_map/concatenate | solution.py:22
  75.6 0.8 fusion.36
  76.9 0.8 fusion.40
  77.8 2.3 %fusion.42 = f32[2,24,256,64]{2,3,1,0:T(8,128)} fusion(bf16[2,69,26,258]{3,1,2,0:T(8,128)(2,1)S(1)} %fusion.18, bf16[3,3,64,69]{3,2,1,0:T(8,128)(2,1)S(1)} %copy-done.3), kind=kOutput, calls=%fused_computation.56 | convolution fusion | flops 108527616 | bytes 4931584 | tf_op jit(solution)/shard_map/oc,pcxy->poxy/dot_general | solution.py:34
  80.0 2.2 %fusion.24 = f32[2,24,256,64]{2,3,1,0:T(8,128)} fusion(bf16[2,69,24,256]{3,1,2,0:T(8,128)(2,1)S(1)} %fusion.44, bf16[2,69,1,256]{3,1,2,0:T(8,128)(2,1)S(1)} %collective-permute-done, bf16[3,3,64,69]{3,2,1,0:T(8,128)(2,1)S(1)} %copy-done.3), kind=kOutput, calls=%fused_computation.38 | convolution fusion | flops 112060416 | bytes 5005312 | tf_op jit(solution)/shard_map/oc,pcxy->poxy/dot_general | solution.py:34
  82.2 2.2 %fusion.28 = f32[2,24,256,64]{2,3,1,0:T(8,128)} fusion(bf16[2,69,1,256]{3,1,2,0:T(8,128)(2,1)S(1)} %collective-permute-done.1, bf16[2,69,24,256]{3,1,2,0:T(8,128)(2,1)S(1)} %fusion.44, bf16[3,3,64,69]{3,2,1,0:T(8,128)(2,1)S(1)} %copy-done.3), kind=kOutput, calls=%fused_computation.42 | convolution fusion | flops 112060416 | bytes 5005312 | tf_op jit(solution)/shard_map/oc,pcxy->poxy/dot_general | solution.py:34
  84.4 6.0 %fusion.15 = bf16[2,64,24,256]{3,1,2,0:T(8,128)(2,1)S(1)} fusion(f32[2,24,256,64]{2,3,1,0:T(8,128)} %fusion.28, f32[2,24,256,64]{2,3,1,0:T(8,128)S(1)} %fusion.34, f32[2,24,256,64]{2,3,1,0:T(8,128)S(1)} %fusion.36, f32[2,24,256,64]{2,3,1,0:T(8,128)} %fusion.111, f32[2,24,256,64]{2,3,1,0:T(8,128)S(1)} %fusion.38, f32[2,24,256,64]{2,3,1,0:T(8,128)S(1)} %fusion.40, ...), kind=kOutput, calls=%fused_computation.27 | convolution fusion | flops 118751232 | bytes 28524544 | tf_op jit(solution)/shard_map/oc,pcxy->poxy/dot_general | solution.py:34
  90.5 1.2 collective-permute-start.2
  91.6 2.7 %collective-permute-start.3 = (bf16[2,64,1,256]{3,1,2,0:T(8,128)(2,1)S(1)}, bf16[2,64,1,256]{3,1,2,0:T(8,128)(2,1)S(1)}, u32[]{:S(2)}, u32[]{:S(2)}) collective-permute-start(bf16[2,64,1,256]{3,1,2,0:T(8,128)(2,1)S(1)} %get-tuple-element.19), channel_id=1, source_target_pairs={{4,0},{8,4},{12,8},{0,12},{5,1},{9,5},{13,9},{1,13},{6,2},{10,6},{... | collective-permute-start | bytes 196616 | tf_op jit(solution)/shard_map/ppermute | solution.py:21
  94.9 1.8 %collective-permute-done.2 = bf16[2,64,1,256]{3,1,2,0:T(8,128)(2,1)S(1)} collective-permute-done((bf16[2,64,1,256]{3,1,2,0:T(8,128)(2,1)S(1)}, bf16[2,64,1,256]{3,1,2,0:T(8,128)(2,1)S(1)}, u32[]{:S(2)}, u32[]{:S(2)}) %collective-permute-start.2) | collective-permute-done | bytes 65568 | tf_op jit(solution)/shard_map/ppermute | solution.py:18
  96.8 1.8 %fusion.23 = bf16[2,64,26,258]{3,1,2,0:T(8,128)(2,1)S(1)} fusion(bf16[2,64,1,256]{3,1,2,0:T(8,128)(2,1)S(1)} %collective-permute-done.3, bf16[2,64,24,256]{3,1,2,0:T(8,128)(2,1)S(1)} %fusion.15, bf16[2,64,1,256]{3,1,2,0:T(8,128)(2,1)S(1)} %collective-permute-done.2), kind=kLoop, calls=%fused_computation.37 | loop fusion | flops 10303488 | bytes 3421184 | tf_op jit(solution)/shard_map/concatenate | solution.py:22
  99.1 0.7 fusion.77
  100.4 2.3 %fusion.81 = f32[2,24,256,64]{2,3,1,0:T(8,128)} fusion(bf16[2,64,26,258]{3,1,2,0:T(8,128)(2,1)S(1)} %fusion.23, bf16[3,3,64,64]{3,2,1,0:T(8,128)(2,1)S(1)} %copy-done.1), kind=kOutput, calls=%fused_computation.91 | convolution fusion | flops 100663296 | bytes 4734976 | tf_op jit(solution)/shard_map/oc,pcxy->poxy/dot_general | solution.py:34
  102.7 2.3 %fusion.85 = f32[2,24,256,64]{2,3,1,0:T(8,128)} fusion(bf16[2,64,26,258]{3,1,2,0:T(8,128)(2,1)S(1)} %fusion.23, bf16[3,3,64,64]{3,2,1,0:T(8,128)(2,1)S(1)} %copy-done.1), kind=kOutput, calls=%fused_computation.96 | convolution fusion | flops 100663296 | bytes 4734976 | tf_op jit(solution)/shard_map/oc,pcxy->poxy/dot_general | solution.py:34
  105.0 2.2 %fusion.83 = f32[2,24,256,64]{2,3,1,0:T(8,128)} fusion(bf16[2,64,24,256]{3,1,2,0:T(8,128)(2,1)S(1)} %fusion.15, bf16[2,64,1,256]{3,1,2,0:T(8,128)(2,1)S(1)} %collective-permute-done.2, bf16[3,3,64,64]{3,2,1,0:T(8,128)(2,1)S(1)} %copy-done.1), kind=kOutput, calls=%fused_computation.94 | convolution fusion | flops 103809024 | bytes 4800512 | tf_op jit(solution)/shard_map/oc,pcxy->poxy/dot_general | solution.py:34
  107.2 2.2 %fusion.73 = f32[2,24,256,64]{2,3,1,0:T(8,128)} fusion(bf16[2,64,1,256]{3,1,2,0:T(8,128)(2,1)S(1)} %collective-permute-done.3, bf16[2,64,24,256]{3,1,2,0:T(8,128)(2,1)S(1)} %fusion.15, bf16[3,3,64,64]{3,2,1,0:T(8,128)(2,1)S(1)} %copy-done.1), kind=kOutput, calls=%fused_computation.83 | convolution fusion | flops 103809024 | bytes 4800512 | tf_op jit(solution)/shard_map/oc,pcxy->poxy/dot_general | solution.py:34
  109.4 5.9 %fusion.16 = bf16[2,64,24,256]{3,1,2,0:T(8,128)(2,1)S(1)} fusion(f32[2,24,256,64]{2,3,1,0:T(8,128)} %fusion.73, f32[2,24,256,64]{2,3,1,0:T(8,128)S(1)} %fusion.75, f32[2,24,256,64]{2,3,1,0:T(8,128)S(1)} %fusion.77, f32[2,24,256,64]{2,3,1,0:T(8,128)S(1)} %fusion.101, f32[2,24,256,64]{2,3,1,0:T(8,128)S(1)} %fusion.79, f32[2,24,256,64]{2,3,1,0:T(8,128)} %fusion.81, ...), kind=kOutput, calls=%fused_computation.28 | convolution fusion | flops 110886912 | bytes 28327936 | tf_op jit(solution)/shard_map/oc,pcxy->poxy/dot_general | solution.py:34
  115.8 3.3 %collective-permute-start.5 = (bf16[2,64,1,256]{3,1,2,0:T(8,128)(2,1)S(1)}, bf16[2,64,1,256]{3,1,2,0:T(8,128)(2,1)S(1)}, u32[]{:S(2)}, u32[]{:S(2)}) collective-permute-start(bf16[2,64,1,256]{3,1,2,0:T(8,128)(2,1)S(1)} %get-tuple-element.17), channel_id=1, source_target_pairs={{4,0},{8,4},{12,8},{0,12},{5,1},{9,5},{13,9},{1,13},{6,2},{10,6},{... | collective-permute-start | bytes 196616 | tf_op jit(solution)/shard_map/ppermute | solution.py:21
  119.2 0.7 fusion.91
  119.9 1.6 collective-permute-done.4
  121.4 1.8 %select_maximum_fusion = bf16[2,64,26,258]{3,1,2,0:T(8,128)(2,1)S(1)} fusion(bf16[2,64,1,256]{3,1,2,0:T(8,128)(2,1)S(1)} %collective-permute-done.5, bf16[2,64,24,256]{3,1,2,0:T(8,128)(2,1)S(1)} %fusion.16, bf16[2,64,1,256]{3,1,2,0:T(8,128)(2,1)S(1)} %collective-permute-done.4), kind=kLoop, calls=%fused_computation.31 | loop fusion | flops 10303488 | bytes 3421184 | tf_op jit(solution)/shard_map/concatenate | solution.py:22
  123.2 2.5 %fusion.59 = f32[2,24,256,69]{2,3,1,0:T(8,128)} fusion(bf16[2,64,26,258]{3,1,2,0:T(8,128)(2,1)S(1)} %select_maximum_fusion, bf16[3,3,69,64]{2,3,1,0:T(8,128)(2,1)S(1)} %copy-done.2), kind=kOutput, calls=%fused_computation.70 | convolution fusion | flops 108527616 | bytes 4980736 | tf_op jit(solution)/shard_map/oc,pcxy->poxy/dot_general | solution.py:34
  125.7 2.6 %fusion.61 = f32[2,24,256,69]{2,3,1,0:T(8,128)} fusion(bf16[2,64,26,258]{3,1,2,0:T(8,128)(2,1)S(1)} %select_maximum_fusion, bf16[3,3,69,64]{2,3,1,0:T(8,128)(2,1)S(1)} %copy-done.2), kind=kOutput, calls=%fused_computation.72 | convolution fusion | flops 108527616 | bytes 4980736 | tf_op jit(solution)/shard_map/oc,pcxy->poxy/dot_general | solution.py:34
  128.3 2.5 %fusion.63 = f32[2,24,256,69]{2,3,1,0:T(8,128)} fusion(bf16[2,64,26,258]{3,1,2,0:T(8,128)(2,1)S(1)} %select_maximum_fusion, bf16[3,3,69,64]{2,3,1,0:T(8,128)(2,1)S(1)} %copy-done.2), kind=kOutput, calls=%fused_computation.74 | convolution fusion | flops 108527616 | bytes 4980736 | tf_op jit(solution)/shard_map/oc,pcxy->poxy/dot_general | solution.py:34
  130.8 2.5 %fusion.65 = f32[2,24,256,69]{2,3,1,0:T(8,128)} fusion(bf16[2,64,26,258]{3,1,2,0:T(8,128)(2,1)S(1)} %select_maximum_fusion, bf16[3,3,69,64]{2,3,1,0:T(8,128)(2,1)S(1)} %copy-done.2), kind=kOutput, calls=%fused_computation.76 | convolution fusion | flops 108527616 | bytes 4980736 | tf_op jit(solution)/shard_map/oc,pcxy->poxy/dot_general | solution.py:34
  133.3 2.4 %fusion.67 = f32[2,24,256,69]{2,3,1,0:T(8,128)} fusion(bf16[2,64,26,258]{3,1,2,0:T(8,128)(2,1)S(1)} %select_maximum_fusion, bf16[3,3,69,64]{2,3,1,0:T(8,128)(2,1)S(1)} %copy-done.2), kind=kOutput, calls=%fused_computation.78 | convolution fusion | flops 108527616 | bytes 4980736 | tf_op jit(solution)/shard_map/oc,pcxy->poxy/dot_general | solution.py:34
  135.7 2.4 %fusion.47 = f32[2,24,256,69]{2,3,1,0:T(8,128)} fusion(bf16[2,64,24,256]{3,1,2,0:T(8,128)(2,1)S(1)} %fusion.16, bf16[2,64,1,256]{3,1,2,0:T(8,128)(2,1)S(1)} %collective-permute-done.4, bf16[3,3,69,64]{2,3,1,0:T(8,128)(2,1)S(1)} %copy-done.2), kind=kOutput, calls=%fused_computation.60 | convolution fusion | flops 111804416 | bytes 5046272 | tf_op jit(solution)/shard_map/oc,pcxy->poxy/dot_general | solution.py:34
  138.1 2.4 %fusion.51 = f32[2,24,256,69]{2,3,1,0:T(8,128)} fusion(bf16[2,64,1,256]{3,1,2,0:T(8,128)(2,1)S(1)} %collective-permute-done.5, bf16[2,64,24,256]{3,1,2,0:T(8,128)(2,1)S(1)} %fusion.16, bf16[3,3,69,64]{2,3,1,0:T(8,128)(2,1)S(1)} %copy-done.2), kind=kOutput, calls=%fused_computation.64 | convolution fusion | flops 111804416 | bytes 5046272 | tf_op jit(solution)/shard_map/oc,pcxy->poxy/dot_general | solution.py:34
  140.5 10.2 %fusion.3 = bf16[2,69,24,256]{3,1,2,0:T(8,128)(2,1)S(1)} fusion(f32[2,24,256,69]{2,3,1,0:T(8,128)} %fusion.51, f32[2,24,256,69]{2,3,1,0:T(8,128)} %fusion.59, f32[2,24,256,69]{2,3,1,0:T(8,128)} %fusion.61, f32[2,24,256,69]{2,3,1,0:T(8,128)S(1)} %fusion.91, f32[2,24,256,69]{2,3,1,0:T(8,128)} %fusion.63, f32[2,24,256,69]{2,3,1,0:T(8,128)} %fusion.65, ...), kind=kOutput, calls=%fused_computation.11 | convolution fusion | flops 122941440 | bytes 34055168 | tf_op jit(solution)/shard_map/oc,pcxy->poxy/dot_general | solution.py:34
  150.7 1.5 copy.21
  (41 shorter events, 4.7 us)
Async XLA Ops:
  7.2 2.2 %copy-start.8 = (u32[32]{0:T(128)S(1)}, u32[32]{0:T(128)}, u32[]{:S(2)}) copy-start(u32[32]{0:T(128)} %constant.60) | copy-start | bytes 388
  7.2 3.4 %copy-start = (bf16[2,69,24,256]{3,2,1,0:T(8,128)(2,1)S(1)}, bf16[2,69,24,256]{3,2,1,0:T(8,128)(2,1)}, u32[]{:S(2)}) copy-start(bf16[2,69,24,256]{3,2,1,0:T(8,128)(2,1)} %param.9) | copy-start | bytes 5087236
  7.2 3.4 %copy-start.5 = (s32[24,256]{1,0:T(8,128)S(1)}, s32[24,256]{1,0:T(8,128)}, u32[]{:S(2)}) copy-start(s32[24,256]{1,0:T(8,128)} %param.12) | copy-start | bytes 73732
  7.2 3.4 %copy-start.4 = (f32[24,256]{1,0:T(8,128)S(1)}, f32[24,256]{1,0:T(8,128)}, u32[]{:S(2)}) copy-start(f32[24,256]{1,0:T(8,128)} %param.11) | copy-start | bytes 73732
  7.2 54.4 %all-gather.3.cloned.1.call-start = ((), (), s32[]{:S(2)}) async-start(), calls=%async_computation | async-start | bytes 8478720 | tf_op jit(solution)/shard_map/all_gather | solution.py:60
  7.9 17.2 %copy-start.7 = (u32[32]{0:T(128)S(1)}, u32[32]{0:T(128)}, u32[]{:S(2)}) copy-start(u32[32]{0:T(128)} %constant.65) | copy-start | bytes 388
  8.0 29.9 %copy-start.6 = (s32[2]{0:T(128)S(1)}, s32[2]{0:T(128)}, u32[]{:S(2)}) copy-start(s32[2]{0:T(128)} %param.13) | copy-start | bytes 28
  65.2 4.4 %copy-start.3 = (bf16[3,3,64,69]{3,2,1,0:T(8,128)(2,1)S(1)}, bf16[3,3,64,69]{3,2,1,0:T(8,128)(2,1)}, u32[]{:S(2)}) copy-start(bf16[3,3,64,69]{3,2,1,0:T(8,128)(2,1)} %param.15) | copy-start | bytes 238468
  65.7 6.7 %collective-permute-start = (bf16[2,69,1,256]{3,1,2,0:T(8,128)(2,1)S(1)}, bf16[2,69,1,256]{3,1,2,0:T(8,128)(2,1)S(1)}, u32[]{:S(2)}, u32[]{:S(2)}) collective-permute-start(bf16[2,69,1,256]{3,1,2,0:T(8,128)(2,1)S(1)} %get-tuple-element.14), channel_id=1, source_target_pairs={{0,4},{4,8},{8,12},{12,0},{1,5},{5,9},{9,13},{13,1},{2,6},{6,10},{... | collective-permute-start | bytes 211976 | tf_op jit(solution)/shard_map/ppermute | solution.py:18
  67.2 5.7 %collective-permute-start.1 = (bf16[2,69,1,256]{3,1,2,0:T(8,128)(2,1)S(1)}, bf16[2,69,1,256]{3,1,2,0:T(8,128)(2,1)S(1)}, u32[]{:S(2)}, u32[]{:S(2)}) collective-permute-start(bf16[2,69,1,256]{3,1,2,0:T(8,128)(2,1)S(1)} %get-tuple-element.15), channel_id=1, source_target_pairs={{4,0},{8,4},{12,8},{0,12},{5,1},{9,5},{13,9},{1,13},{6,2},{10,6},{... | collective-permute-start | bytes 211976 | tf_op jit(solution)/shard_map/ppermute | solution.py:21
  84.4 9.9 %copy-start.1 = (bf16[3,3,64,64]{3,2,1,0:T(8,128)(2,1)S(1)}, bf16[3,3,64,64]{3,2,1,0:T(8,128)(2,1)}, u32[]{:S(2)}) copy-start(bf16[3,3,64,64]{3,2,1,0:T(8,128)(2,1)} %param.16) | copy-start | bytes 221188
  90.5 6.3 %collective-permute-start.2 = (bf16[2,64,1,256]{3,1,2,0:T(8,128)(2,1)S(1)}, bf16[2,64,1,256]{3,1,2,0:T(8,128)(2,1)S(1)}, u32[]{:S(2)}, u32[]{:S(2)}) collective-permute-start(bf16[2,64,1,256]{3,1,2,0:T(8,128)(2,1)S(1)} %get-tuple-element.18), channel_id=1, source_target_pairs={{0,4},{4,8},{8,12},{12,0},{1,5},{5,9},{9,13},{13,1},{2,6},{6,10},{... | collective-permute-start | bytes 196616 | tf_op jit(solution)/shard_map/ppermute | solution.py:18
  91.6 5.2 %collective-permute-start.3 = (bf16[2,64,1,256]{3,1,2,0:T(8,128)(2,1)S(1)}, bf16[2,64,1,256]{3,1,2,0:T(8,128)(2,1)S(1)}, u32[]{:S(2)}, u32[]{:S(2)}) collective-permute-start(bf16[2,64,1,256]{3,1,2,0:T(8,128)(2,1)S(1)} %get-tuple-element.19), channel_id=1, source_target_pairs={{4,0},{8,4},{12,8},{0,12},{5,1},{9,5},{13,9},{1,13},{6,2},{10,6},{... | collective-permute-start | bytes 196616 | tf_op jit(solution)/shard_map/ppermute | solution.py:21
  109.4 9.8 %copy-start.2 = (bf16[3,3,69,64]{2,3,1,0:T(8,128)(2,1)S(1)}, bf16[3,3,69,64]{2,3,1,0:T(8,128)(2,1)}, u32[]{:S(2)}) copy-start(bf16[3,3,69,64]{2,3,1,0:T(8,128)(2,1)} %param.17) | copy-start | bytes 238468
  115.3 6.2 %collective-permute-start.4 = (bf16[2,64,1,256]{3,1,2,0:T(8,128)(2,1)S(1)}, bf16[2,64,1,256]{3,1,2,0:T(8,128)(2,1)S(1)}, u32[]{:S(2)}, u32[]{:S(2)}) collective-permute-start(bf16[2,64,1,256]{3,1,2,0:T(8,128)(2,1)S(1)} %get-tuple-element.16), channel_id=1, source_target_pairs={{0,4},{4,8},{8,12},{12,0},{1,5},{5,9},{9,13},{13,1},{2,6},{6,10},{... | collective-permute-start | bytes 196616 | tf_op jit(solution)/shard_map/ppermute | solution.py:18
  115.8 5.6 %collective-permute-start.5 = (bf16[2,64,1,256]{3,1,2,0:T(8,128)(2,1)S(1)}, bf16[2,64,1,256]{3,1,2,0:T(8,128)(2,1)S(1)}, u32[]{:S(2)}, u32[]{:S(2)}) collective-permute-start(bf16[2,64,1,256]{3,1,2,0:T(8,128)(2,1)S(1)} %get-tuple-element.17), channel_id=1, source_target_pairs={{4,0},{8,4},{12,8},{0,12},{5,1},{9,5},{13,9},{1,13},{6,2},{10,6},{... | collective-permute-start | bytes 196616 | tf_op jit(solution)/shard_map/ppermute | solution.py:21
Sparse Core Ops, SparseCore 0:
  9.6 51.9 all-gather.2
